TPU v7x, 32 devices: a whole 2x2x4 slice. The times are simulated.
32 devices in a mesh: gx: 8 (over z, core), gy: 4 (over y, x).
Axes of the slice: x: 2, y: 2, z: 4, core: 2. Of those that a mesh axis runs over, the one named last changes fastest.
Arguments:
- diag_blocks: bfloat16 [32, 64, 128, 128], P('gy', 'gx'), may hold values from -0.13 to 4.25
- edge_blocks: bfloat16 [32, 64, 2, 128, 128], P('gy', 'gx'), may hold values from -1.8 to 0.13
- left_pick: int32 [32, 8], P('gy', 'gx'), may hold values from -4 to 4
- right_pick: int32 [32, 8], P('gy', 'gx'), may hold values from -4 to 4
Outputs:
- pivots: bfloat16 [32, 96, 128, 128], P('gy', 'gx')
- multipliers: bfloat16 [32, 88, 128, 128], P('gy', 'gx')
All inputs are finite; a program needn't handle non-finite values.
Results may differ from a plain program's by a relative error of at most 0.0011.
Values may be sent and summed in bfloat16 or wider, within the bound.
A program may use at most 128 MiB of HBM per device.

v0:
```python
import jax
import jax.numpy as jnp
from jax import lax
from jax.sharding import PartitionSpec as P

REACH = 4


def shifted(array, axis, by):
    peers = lax.axis_size(axis)
    return lax.ppermute(array, axis, [(i, (i + by) % peers) for i in range(peers)])


def extended(cells, sides, width):
    for axis, dim in sides:
        count = lax.axis_size(axis)
        ends = count - 1
        head = lax.slice_in_dim(cells, 0, width, axis=dim)
        tail = lax.slice_in_dim(cells, cells.shape[dim] - width, cells.shape[dim], axis=dim)
        cells = jnp.concatenate(
            [
                lax.ppermute(tail, axis, [(i, (i + 1) % count) for i in range(ends)]),
                cells,
                lax.ppermute(head, axis, [((i + 1) % count, i) for i in range(ends)]),
            ],
            axis=dim,
        )
    return cells


def newton(schur):
    size = schur.shape[-1]
    eye = jnp.eye(size, dtype=schur.dtype)
    inverse_diag = 1.0 / jnp.diagonal(schur, axis1=-2, axis2=-1)
    first = (
        2.0 * eye * inverse_diag[..., None, :]
        - inverse_diag[..., :, None] * schur * inverse_diag[..., None, :]
    )
    inner = jnp.einsum("bij,bjk->bik", schur, first, precision=lax.Precision.HIGHEST)
    return 2.0 * first - jnp.einsum("bij,bjk->bik", first, inner, precision=lax.Precision.HIGHEST)


def factor(band_diag, upper, lower):
    start = newton(band_diag[:, 0])

    def advance(previous, items):
        block, up_link, low_link = items
        mult = jnp.einsum("bij,bjk->bik", low_link, previous, precision=lax.Precision.HIGHEST)
        schur = block - jnp.einsum("bij,bjk->bik", mult, up_link, precision=lax.Precision.HIGHEST)
        pivot = newton(schur)
        return (pivot, (pivot, mult))

    items = (
        jnp.moveaxis(band_diag[:, 1:], 1, 0),
        jnp.moveaxis(upper, 1, 0),
        jnp.moveaxis(lower, 1, 0),
    )
    _, (later, mults) = lax.scan(advance, start, items)
    pivots = jnp.concatenate([start[:, None], jnp.moveaxis(later, 0, 1)], axis=1)
    return (pivots.astype(jnp.bfloat16), jnp.moveaxis(mults, 0, 1).astype(jnp.bfloat16))


def on_device(diag_blocks, edge_blocks, left_pick, right_pick):
    lines = diag_blocks.shape[0]
    tiles = diag_blocks.shape[1]
    size = diag_blocks.shape[2]
    tail_edges = edge_blocks[:, tiles - 2 :].reshape(lines, 4, size, size)
    to_next = jnp.concatenate([diag_blocks[:, tiles - 2 :], tail_edges], axis=1)
    to_prev = jnp.concatenate([diag_blocks[:, :2], edge_blocks[:, 0]], axis=1)
    from_prev = shifted(to_next, "gx", 1)
    from_next = shifted(to_prev, "gx", -1)
    joined = jnp.concatenate([from_prev, from_next], axis=1)
    window = extended(joined, (("gy", 0),), REACH)
    row_count = lines * lax.axis_size("gy")
    first_row = lax.axis_index("gy") * lines
    own_rows = first_row + jnp.arange(lines, dtype=jnp.int32)
    left_at = jnp.clip(own_rows + left_pick[:, 0], 0, row_count - 1) - first_row + REACH
    right_at = jnp.clip(own_rows + right_pick[:, 0], 0, row_count - 1) - first_row + REACH
    left_rim = jnp.take(window[:, :6], left_at, axis=0)
    right_rim = jnp.take(window[:, 6:], right_at, axis=0)
    band_diag = jnp.concatenate([left_rim[:, :2], diag_blocks, right_rim[:, :2]], axis=1).astype(
        jnp.float32
    )
    left_links = left_rim[:, 2:].reshape(lines, 2, 2, size, size)
    links = jnp.concatenate([left_links, edge_blocks, right_rim[:, 2:][:, None]], axis=1)
    upper = links[:, :, 0].astype(jnp.float32)
    lower = links[:, :, 1].astype(jnp.float32)
    return factor(band_diag, upper, lower)


def solution(mesh):
    return jax.shard_map(
        on_device,
        mesh=mesh,
        in_specs=(
            P("gy", "gx", None, None),
            P("gy", "gx", None, None, None),
            P("gy", "gx"),
            P("gy", "gx"),
        ),
        out_specs=(P("gy", "gx", None, None), P("gy", "gx", None, None)),
        check_vma=False,
    )
```

profile of v0, /device:TPU:19, one launch (start us, length us, event | category | flops | bytes accessed | tf_op | source)
XLA Modules:
  0.0 283.9 jit_solution(16396045293412181891)
XLA Ops:
  2.3 1.9 collective-permute-start
  5.1 27.7 %collective-permute-done = bf16[8,6,128,128]{3,2,1,0:T(8,128)(2,1)S(1)} collective-permute-done((bf16[8,6,128,128]{3,2,1,0:T(8,128)(2,1)S(1)}, bf16[8,6,128,128]{3,2,1,0:T(8,128)(2,1)S(1)}, u32[]{:S(2)}, u32[]{:S(2)}) %collective-permute-start) | collective-permute-done | bytes 1572896 | tf_op jit(solution)/shard_map/ppermute | solution.py:11
  34.9 3.1 %collective-permute-start.2 = (bf16[4,10,128,128]{3,2,1,0:T(8,128)(2,1)}, bf16[4,10,128,128]{3,2,1,0:T(8,128)(2,1)}, u32[]{:S(2)}, u32[]{:S(2)}) collective-permute-start(bf16[4,10,128,128]{3,2,1,0:T(8,128)(2,1)} %get-tuple-element.68), channel_id=1, source_target_pairs={{0,1},{1,2},{2,3},{4,5},{5,6},{6,7},{8,9},{9,10},{10,11},{12,13},{... | collective-permute-start | bytes 3932168 | tf_op jit(solution)/shard_map/ppermute | solution.py:22
  38.0 3.2 %collective-permute-start.3 = (bf16[4,10,128,128]{3,2,1,0:T(8,128)(2,1)}, bf16[4,10,128,128]{3,2,1,0:T(8,128)(2,1)}, u32[]{:S(2)}, u32[]{:S(2)}) collective-permute-start(bf16[4,10,128,128]{3,2,1,0:T(8,128)(2,1)} %get-tuple-element.69), channel_id=1, source_target_pairs={{1,0},{2,1},{3,2},{5,4},{6,5},{7,6},{9,8},{10,9},{11,10},{13,12},{... | collective-permute-start | bytes 3932168 | tf_op jit(solution)/shard_map/ppermute | solution.py:24
  41.4 24.7 %collective-permute-done.2 = bf16[4,10,128,128]{3,2,1,0:T(8,128)(2,1)} collective-permute-done((bf16[4,10,128,128]{3,2,1,0:T(8,128)(2,1)}, bf16[4,10,128,128]{3,2,1,0:T(8,128)(2,1)}, u32[]{:S(2)}, u32[]{:S(2)}) %collective-permute-start.2) | collective-permute-done | bytes 1310752 | tf_op jit(solution)/shard_map/ppermute | solution.py:22
  66.1 29.0 %collective-permute-done.3 = bf16[4,10,128,128]{3,2,1,0:T(8,128)(2,1)} collective-permute-done((bf16[4,10,128,128]{3,2,1,0:T(8,128)(2,1)}, bf16[4,10,128,128]{3,2,1,0:T(8,128)(2,1)}, u32[]{:S(2)}, u32[]{:S(2)}) %collective-permute-start.3) | collective-permute-done | bytes 1310752 | tf_op jit(solution)/shard_map/ppermute | solution.py:24
  95.1 2.3 pad_maximum_fusion.1
  97.5 1.9 slice.79
  99.3 3.8 %gather_fusion.1 = bf16[8,6,128,128]{3,2,1,0:T(8,128)(2,1)} fusion(bf16[16,6,128,128]{3,2,1,0:T(8,128)(2,1)} %slice.79, s32[1024]{0:T(1024)S(1)} %pad_clamp_fusion.1), kind=kCustom, calls=%fused_computation.1 | custom fusion | bytes 3145760 | tf_op jit(solution)/shard_map/jit(_take)/gather | solution.py:79
  106.0 2.8 pad_maximum_fusion.5
  108.7 3.4 %gather_fusion.2 = bf16[8,4,128,128]{3,2,1,0:T(8,128)(2,1)} fusion(bf16[16,4,128,128]{3,2,1,0:T(8,128)(2,1)} %pad_maximum_fusion.5, s32[1024]{0:T(1024)S(1)} %pad_clamp_fusion), kind=kCustom, calls=%fused_computation.2 | custom fusion | bytes 2097184 | tf_op jit(solution)/shard_map/jit(_take)/gather | solution.py:80
  115.3 3.3 %convert_bitcast_fusion.2 = f32[11,8,128,128]{3,2,1,0:T(8,128)} fusion(bf16[8,2,128,128]{3,2,0,1:T(8,128)(2,1)S(1)} %get-tuple-element.73, bf16[8,2,128,128]{3,2,0,1:T(8,128)(2,1)S(1)} %slice.80, bf16[8,8,128,128]{3,2,1,0:T(8,128)(2,1)S(1)} %copy-done), kind=kLoop, calls=%fused_computation.30 | loop fusion | flops 8650752 | bytes 8912896 | tf_op jit(solution)/shard_map/transpose | solution.py:54
  118.6 6.0 %copy.26 = f32[8,128,128]{0,2,1:T(8,128)} copy(f32[8,128,128]{2,1,0:T(8,128)} %get-tuple-element.56) | data formatting | bytes 1048576 | tf_op jit(solution)/shard_map/squeeze | solution.py:44
  127.9 3.3 %pad_maximum_fusion = bf16[8,11,2,128,128]{4,3,0,1,2:T(8,128)(2,1)S(1)} fusion(bf16[8,1,2,128,128]{4,3,0,1,2:T(8,128)(2,1)} %get-tuple-element.72, bf16[8,2,2,128,128]{4,3,0,2,1:T(8,128)(2,1)S(1)} %bitcast.110, bf16[8,8,2,128,128]{4,3,2,1,0:T(8,128)(2,1)} %param.7), kind=kLoop, calls=%fused_computation.27 | loop fusion | flops 17301504 | bytes 11534336 | tf_op jit(solution)/shard_map/concatenate | solution.py:85
  131.2 5.8 %convert_bitcast_fusion = (f32[11,8,128,128]{3,2,1,0:T(8,128)}, f32[11,8,128,128]{3,2,1,0:T(8,128)}) fusion(bf16[8,11,2,128,128]{4,3,0,1,2:T(8,128)(2,1)S(1)} %pad_maximum_fusion), kind=kLoop, calls=%fused_computation.28 | loop fusion | flops 2883584 | bytes 17301504 | tf_op jit(solution)/shard_map/transpose | solution.py:55
  137.0 143.1 %while.14 = (s32[]{:T(128)}, f32[8,128,128]{2,1,0:T(8,128)S(1)}, bf16[11,8,128,128]{3,2,0,1:T(8,128)(2,1)}, bf16[11,8,128,128]{3,2,0,1:T(8,128)(2,1)}, f32[11,8,...) while((s32[]{:T(128)}, f32[8,128,128]{2,1,0:T(8,128)S(1)}, ...), condition=%wide.region_1.2_spmd, body=%wide.region_0.1_spmd.sunk | while | flops 807306752 | bytes 9224277 | solution.py:58
  137.0 2.4 bitcast_dynamic-update-slice_fusion.4
  139.4 1.8 convolution_subtract_fusion.4
  141.3 4.6 %copy.52 = f32[8,128,128]{0,2,1:T(8,128)} copy(f32[8,128,128]{2,1,0:T(8,128)S(1)} %convolution_subtract_fusion.4) | data formatting | bytes 1048576 | tf_op jit(solution)/shard_map/while/body/eval_jaxpr/sub | solution.py:49
  150.0 2.4 bitcast_dynamic-update-slice_fusion.4
  152.4 1.8 convolution_subtract_fusion.4
  154.3 4.6 %copy.52 = f32[8,128,128]{0,2,1:T(8,128)} copy(f32[8,128,128]{2,1,0:T(8,128)S(1)} %convolution_subtract_fusion.4) | data formatting | bytes 1048576 | tf_op jit(solution)/shard_map/while/body/eval_jaxpr/sub | solution.py:49
  163.0 2.4 bitcast_dynamic-update-slice_fusion.4
  165.4 1.8 convolution_subtract_fusion.4
  167.3 4.6 %copy.52 = f32[8,128,128]{0,2,1:T(8,128)} copy(f32[8,128,128]{2,1,0:T(8,128)S(1)} %convolution_subtract_fusion.4) | data formatting | bytes 1048576 | tf_op jit(solution)/shard_map/while/body/eval_jaxpr/sub | solution.py:49
  176.0 2.4 bitcast_dynamic-update-slice_fusion.4
  178.4 1.8 convolution_subtract_fusion.4
  180.3 4.6 %copy.52 = f32[8,128,128]{0,2,1:T(8,128)} copy(f32[8,128,128]{2,1,0:T(8,128)S(1)} %convolution_subtract_fusion.4) | data formatting | bytes 1048576 | tf_op jit(solution)/shard_map/while/body/eval_jaxpr/sub | solution.py:49
  189.1 2.4 bitcast_dynamic-update-slice_fusion.4
  191.4 1.8 convolution_subtract_fusion.4
  193.3 4.6 %copy.52 = f32[8,128,128]{0,2,1:T(8,128)} copy(f32[8,128,128]{2,1,0:T(8,128)S(1)} %convolution_subtract_fusion.4) | data formatting | bytes 1048576 | tf_op jit(solution)/shard_map/while/body/eval_jaxpr/sub | solution.py:49
  202.1 2.4 bitcast_dynamic-update-slice_fusion.4
  204.5 1.8 convolution_subtract_fusion.4
  206.3 4.6 %copy.52 = f32[8,128,128]{0,2,1:T(8,128)} copy(f32[8,128,128]{2,1,0:T(8,128)S(1)} %convolution_subtract_fusion.4) | data formatting | bytes 1048576 | tf_op jit(solution)/shard_map/while/body/eval_jaxpr/sub | solution.py:49
  215.1 2.4 bitcast_dynamic-update-slice_fusion.4
  217.5 1.8 convolution_subtract_fusion.4
  219.4 4.6 %copy.52 = f32[8,128,128]{0,2,1:T(8,128)} copy(f32[8,128,128]{2,1,0:T(8,128)S(1)} %convolution_subtract_fusion.4) | data formatting | bytes 1048576 | tf_op jit(solution)/shard_map/while/body/eval_jaxpr/sub | solution.py:49
  228.1 2.4 bitcast_dynamic-update-slice_fusion.4
  230.5 1.8 convolution_subtract_fusion.4
  232.4 4.6 %copy.52 = f32[8,128,128]{0,2,1:T(8,128)} copy(f32[8,128,128]{2,1,0:T(8,128)S(1)} %convolution_subtract_fusion.4) | data formatting | bytes 1048576 | tf_op jit(solution)/shard_map/while/body/eval_jaxpr/sub | solution.py:49
  241.1 2.4 bitcast_dynamic-update-slice_fusion.4
  243.5 1.8 convolution_subtract_fusion.4
  245.4 4.6 %copy.52 = f32[8,128,128]{0,2,1:T(8,128)} copy(f32[8,128,128]{2,1,0:T(8,128)S(1)} %convolution_subtract_fusion.4) | data formatting | bytes 1048576 | tf_op jit(solution)/shard_map/while/body/eval_jaxpr/sub | solution.py:49
  254.2 2.4 bitcast_dynamic-update-slice_fusion.4
  258.4 4.6 %copy.52 = f32[8,128,128]{0,2,1:T(8,128)} copy(f32[8,128,128]{2,1,0:T(8,128)S(1)} %convolution_subtract_fusion.4) | data formatting | bytes 1048576 | tf_op jit(solution)/shard_map/while/body/eval_jaxpr/sub | solution.py:49
  267.2 2.4 bitcast_dynamic-update-slice_fusion.4
  271.4 4.6 %copy.52 = f32[8,128,128]{0,2,1:T(8,128)} copy(f32[8,128,128]{2,1,0:T(8,128)S(1)} %convolution_subtract_fusion.4) | data formatting | bytes 1048576 | tf_op jit(solution)/shard_map/while/body/eval_jaxpr/sub | solution.py:49
  280.1 3.7 %pad_maximum_fusion.2 = bf16[8,12,128,128]{3,2,1,0:T(8,128)(2,1)} fusion(bf16[8,11,128,128]{3,2,1,0:T(8,128)(2,1)} %bitcast.111, bf16[8,1,128,128]{3,2,1,0:T(8,128)(2,1)S(1)} %convert_bitcast_fusion.8), kind=kLoop, calls=%fused_computation.32 | loop fusion | flops 1572864 | bytes 6291456 | tf_op jit(solution)/shard_map/concatenate | solution.py:59
  (123 shorter events, 63.1 us)
Async XLA Ops:
  0.6 1.5 slice-start
  2.0 2.2 copy-start.1
  2.3 30.5 %collective-permute-start = (bf16[8,6,128,128]{3,2,1,0:T(8,128)(2,1)S(1)}, bf16[8,6,128,128]{3,2,1,0:T(8,128)(2,1)S(1)}, u32[]{:S(2)}, u32[]{:S(2)}) collective-permute-start(bf16[8,6,128,128]{3,2,1,0:T(8,128)(2,1)S(1)} %pad_maximum_fusion.6), channel_id=1, source_target_pairs={{0,4},{4,8},{8,12},{12,16},{16,20},{20,24},{24,28},{28,0},{1,5},{5... | collective-permute-start | bytes 4718600 | tf_op jit(solution)/shard_map/ppermute | solution.py:11
  4.4 28.6 %collective-permute-start.1 = (bf16[8,4,128,128]{3,2,1,0:T(8,128)(2,1)S(1)}, bf16[8,4,128,128]{3,2,1,0:T(8,128)(2,1)S(1)}, u32[]{:S(2)}, u32[]{:S(2)}) collective-permute-start(bf16[8,4,128,128]{3,2,1,0:T(8,128)(2,1)S(1)} %pad_maximum_fusion.7), channel_id=1, source_target_pairs={{0,28},{4,0},{8,4},{12,8},{16,12},{20,16},{24,20},{28,24},{1,29},{... | collective-permute-start | bytes 3145736 | tf_op jit(solution)/shard_map/ppermute | solution.py:11
  33.1 8.1 %copy-start.4 = (s32[8,1]{0,1:T(1,128)S(1)}, s32[8,1]{0,1:T(1,128)}, u32[]{:S(2)}) copy-start(s32[8,1]{0,1:T(1,128)} %param.8) | copy-start | bytes 100
  33.2 8.1 %copy-start.5 = (s32[8,1]{0,1:T(1,128)S(1)}, s32[8,1]{0,1:T(1,128)}, u32[]{:S(2)}) copy-start(s32[8,1]{0,1:T(1,128)} %param.9) | copy-start | bytes 100
  34.9 31.2 %collective-permute-start.2 = (bf16[4,10,128,128]{3,2,1,0:T(8,128)(2,1)}, bf16[4,10,128,128]{3,2,1,0:T(8,128)(2,1)}, u32[]{:S(2)}, u32[]{:S(2)}) collective-permute-start(bf16[4,10,128,128]{3,2,1,0:T(8,128)(2,1)} %get-tuple-element.68), channel_id=1, source_target_pairs={{0,1},{1,2},{2,3},{4,5},{5,6},{6,7},{8,9},{9,10},{10,11},{12,13},{... | collective-permute-start | bytes 3932168 | tf_op jit(solution)/shard_map/ppermute | solution.py:22
  38.0 57.2 %collective-permute-start.3 = (bf16[4,10,128,128]{3,2,1,0:T(8,128)(2,1)}, bf16[4,10,128,128]{3,2,1,0:T(8,128)(2,1)}, u32[]{:S(2)}, u32[]{:S(2)}) collective-permute-start(bf16[4,10,128,128]{3,2,1,0:T(8,128)(2,1)} %get-tuple-element.69), channel_id=1, source_target_pairs={{1,0},{2,1},{3,2},{5,4},{6,5},{7,6},{9,8},{10,9},{11,10},{13,12},{... | collective-permute-start | bytes 3932168 | tf_op jit(solution)/shard_map/ppermute | solution.py:24
  104.8 1.2 copy-start.2
  108.7 5.7 %copy-start = (bf16[8,8,128,128]{3,2,1,0:T(8,128)(2,1)S(1)}, bf16[8,8,128,128]{3,2,1,0:T(8,128)(2,1)}, u32[]{:S(2)}) copy-start(bf16[8,8,128,128]{3,2,1,0:T(8,128)(2,1)} %param.6) | copy-start | bytes 6291460
  118.6 7.9 %copy-start.3 = (bf16[8,6,128,128]{3,2,0,1:T(8,128)(2,1)S(1)}, bf16[8,6,128,128]{3,2,0,1:T(8,128)(2,1)}, u32[]{:S(2)}) copy-start(bf16[8,6,128,128]{3,2,0,1:T(8,128)(2,1)} %copy-done.2) | copy-start | bytes 4718596
  126.4 1.6 slice-start.1
where the time goes:
time: 288 us; the launch traced here: 284 us
  local copies, waits for them, and re-layouts  93.2 us (32%)
  waiting for transfers between devices  81.5 us (28%)
  matrix products  72.9 us (25%)
  other arithmetic  26 us (9%)
  starting transfers between devices  8.98 us (3%)
    sub x11, local copies, waits for them, and re-layouts, advance(): block - jnp.einsum('bij,bjk->bik', mult, up_link, precision=lax.Precision...  50.7 us
    ppermute x1, waiting for transfers between devices, extended(): lax.ppermute(head, axis, [((i + 1) % count, i) for i in range(ends)])  29 us
    ppermute x2, waiting for transfers between devices, shifted(): lax.ppermute(array, axis, [(i, (i + by) % peers) for i in range(peers)])  27.7 us
    dot_general x11, matrix products, advance(): jnp.einsum('bij,bjk->bik', low_link, previous, precision=lax.Precision.HI...  26.3 us
    ppermute x1, waiting for transfers between devices, extended(): lax.ppermute(tail, axis, [(i, (i + 1) % count) for i in range(ends)])  24.7 us
    gather x12, local copies, waits for them, and re-layouts, newton(): inverse_diag = 1.0 / jnp.diagonal(schur, axis1=-2, axis2=-1)  21.2 us
    dot_general x11, matrix products, advance(): jnp.einsum('bij,bjk->bik', mult, up_link, precision=lax.Precision.HIGHEST)  20.2 us
    dot_general x12, matrix products, newton(): jnp.einsum('bij,bjk->bik', first, inner, precision=lax.Precision.HIGHEST)  17.8 us
  transfers between devices with their start and end apart: 4, of which 3 were waited for; matrix products, arithmetic and copies ran while one was open for 0% of the time, Pallas kernels for 0%

commit v1 on v0

v1 whole, which is shorter than its diff:
```python
import functools

import jax
import jax.numpy as jnp
from jax import lax
from jax.experimental import pallas as pl
from jax.experimental.pallas import tpu as pltpu
from jax.sharding import PartitionSpec as P

F32 = jnp.float32
BF16 = jnp.bfloat16
MESH = pl.DeviceIdType.MESH


def dot(a, b):
    return lax.dot_general(a, b, (((1,), (0,)), ((), ())), preferred_element_type=F32)


def split(x):
    high = x.astype(BF16)
    return high, (x - high.astype(F32)).astype(BF16)


def wide(*parts):
    return jnp.concatenate(parts, axis=1)


def tall(*parts):
    return jnp.concatenate(parts, axis=0)


def newton_all(schurs):
    size = schurs[0].shape[-1]
    rows = lax.broadcasted_iota(jnp.int32, (size, size), 0)
    cols = lax.broadcasted_iota(jnp.int32, (size, size), 1)
    on = rows == cols
    state = []
    for s in schurs:
        d_row = 1.0 / jnp.sum(jnp.where(on, s, 0.0), axis=0, keepdims=True)
        r = jnp.where(on, 0.0, s) * d_row
        rh, rl = split(r)
        state.append((d_row, r, rh, rl))
    squares = [dot(wide(rh, rl), tall(rh, rh)) + dot(rh, rl) for _, _, rh, rl in state]
    out = []
    for (d_row, r, rh, rl), r2 in zip(state, squares):
        sh, sl = split(r2)
        r3 = dot(wide(rh, rl), tall(sh, sh)) + dot(rh, sl)
        d_col = jnp.sum(jnp.where(on, d_row, 0.0), axis=1, keepdims=True)
        out.append(d_col * (jnp.where(on, 1.0, 0.0) - r + r2 - r3))
    return out


def times_link(low, stacked):
    return dot(wide(low, low), stacked)


def times_exact(m, up):
    mh, ml = split(m)
    return dot(wide(mh, ml), tall(up, up))


def stack_split(p):
    return tall(*split(p))


def pick(j, i, half, own, prev, nxt):
    lines = 2 * half
    value = own[jnp.clip(j, 0, lines - 1)]
    if i < half:
        return jnp.where(j < 0, prev[jnp.clip(j + half, 0, half - 1)], value)
    return jnp.where(j >= lines, nxt[jnp.clip(j - lines, 0, half - 1)], value)


def advance(blocks, ups, lows, stacked):
    group = range(len(blocks))
    m = [times_link(lows[i], stacked[i]) for i in group]
    s = [blocks[i].astype(F32) - times_exact(m[i], ups[i]) for i in group]
    return m, newton_all(s)


def kernel(
    left_pick, right_pick, diag, edge, piv, mul,
    dv, ev, carry,
    c_out, cd_out, r_out,
    c_own, cd_own, r_own, hd_own, he_own,
    c_prev, cd_prev, r_prev, hd_prev, he_prev,
    c_next, cd_next, r_next, hd_next, he_next,
    local_sem, send_x, recv_x, send_y, recv_y,
):
    lines, tiles, size, _ = dv.shape
    half = lines // 2
    group = range(lines)
    gx, gy = lax.axis_index("gx"), lax.axis_index("gy")
    nx, ny = lax.axis_size("gx"), lax.axis_size("gy")
    ahead, behind = lax.rem(gx + 1, nx), lax.rem(gx + nx - 1, nx)
    has_prev, has_next = gy > 0, gy < ny - 1
    up, down = jnp.maximum(gy - 1, 0), jnp.minimum(gy + 1, ny - 1)
    halves = (pl.ds(0, half), pl.ds(half, half))

    def local(n, a, b):
        return pltpu.make_async_copy(a, b, local_sem.at[n])

    loads = [
        local(0, diag.at[:, pl.ds(tiles - 2, 2)], dv.at[:, pl.ds(tiles - 2, 2)]),
        local(1, edge.at[:, pl.ds(tiles - 2, 2)], ev.at[:, pl.ds(tiles - 2, 2)]),
        local(2, diag.at[:, pl.ds(0, tiles - 2)], dv.at[:, pl.ds(0, tiles - 2)]),
        local(3, edge.at[:, pl.ds(0, tiles - 2)], ev.at[:, pl.ds(0, tiles - 2)]),
    ]
    for copy in loads:
        copy.start()

    def to_x(n, a, b, x):
        return pltpu.make_async_remote_copy(
            src_ref=a, dst_ref=b, send_sem=send_x.at[n], recv_sem=recv_x.at[n],
            device_id=(x, gy), device_id_type=MESH,
        )

    def to_y(n, a, b, y):
        return pltpu.make_async_remote_copy(
            src_ref=a, dst_ref=b, send_sem=send_y.at[n], recv_sem=recv_y.at[n],
            device_id=(gx, y), device_id_type=MESH,
        )

    heads_x = [
        copy
        for h, part in enumerate(halves)
        for copy in (
            to_x(2 * h, diag.at[part, pl.ds(0, 2)], hd_own.at[part], behind),
            to_x(2 * h + 1, edge.at[part, 0], he_own.at[part], behind),
        )
    ]
    start_x = [to_x(4, cd_out, cd_own, ahead)] + [
        to_x(5 + h, c_out.at[part], c_own.at[part], ahead) for h, part in enumerate(halves)
    ]
    rims_x = [to_x(7 + h, r_out.at[part], r_own.at[part], ahead) for h, part in enumerate(halves)]

    low, high = halves
    start_y = (
        [to_y(0, cd_own.at[low], cd_next, up), to_y(1, c_own.at[low], c_next, up)],
        [to_y(2, cd_own.at[high], cd_prev, down), to_y(3, c_own.at[high], c_prev, down)],
    )
    heads_y = (
        [to_y(4, hd_own.at[low], hd_next, up), to_y(5, he_own.at[low], he_next, up)],
        [to_y(6, hd_own.at[high], hd_prev, down), to_y(7, he_own.at[high], he_prev, down)],
    )
    rims_y = ([to_y(8, r_own.at[low], r_next, up)], [to_y(9, r_own.at[high], r_prev, down)])

    def forward(copies):
        @pl.when(has_prev)
        def _():
            for copy in copies[0]:
                copy.start()

        @pl.when(has_next)
        def _():
            for copy in copies[1]:
                copy.start()

    def receive(copies):
        @pl.when(has_next)
        def _():
            for copy in copies[0]:
                copy.wait_recv()

        @pl.when(has_prev)
        def _():
            for copy in copies[1]:
                copy.wait_recv()

    def drain(copies):
        @pl.when(has_prev)
        def _():
            for copy in copies[0]:
                copy.wait_send()

        @pl.when(has_next)
        def _():
            for copy in copies[1]:
                copy.wait_send()

    barrier = pltpu.get_barrier_semaphore()
    for x in (ahead, behind):
        pl.semaphore_signal(barrier, inc=1, device_id=(x, gy), device_id_type=MESH)

    @pl.when(has_prev)
    def _():
        pl.semaphore_signal(barrier, inc=1, device_id=(gx, up), device_id_type=MESH)

    @pl.when(has_next)
    def _():
        pl.semaphore_signal(barrier, inc=1, device_id=(gx, down), device_id_type=MESH)

    pl.semaphore_wait(barrier, 2 + has_prev.astype(jnp.int32) + has_next.astype(jnp.int32))

    for copy in heads_x:
        copy.start()

    loads[0].wait()
    loads[1].wait()
    on = lax.broadcasted_iota(jnp.int32, (size, size), 0) == lax.broadcasted_iota(
        jnp.int32, (size, size), 1
    )
    t0, t1 = tiles - 2, tiles - 1
    p = newton_all([dv[i, t0].astype(F32) for i in group])
    m = [times_link(ev[i, t0, 1], stack_split(p[i])) for i in group]
    for i in group:
        r_out[i, 0] = p[i].astype(BF16)
        r_out[i, 2] = m[i].astype(BF16)
    p = newton_all([dv[i, t1].astype(F32) - times_exact(m[i], ev[i, t0, 0]) for i in group])
    m = [times_link(ev[i, t1, 1], stack_split(p[i])) for i in group]
    c = [times_exact(m[i], ev[i, t1, 0]) for i in group]
    for i in group:
        c_out[i] = c[i].astype(BF16)
        cd_out[i] = jnp.broadcast_to(
            jnp.sum(jnp.where(on, c[i], 0.0), axis=0, keepdims=True), cd_out.shape[1:]
        )
    for i in group:
        r_out[i, 1] = p[i].astype(BF16)
        r_out[i, 3] = m[i].astype(BF16)
    for copy in start_x + rims_x:
        copy.start()

    for copy in start_x:
        copy.wait_recv()
    forward(start_y)
    for copy in heads_x:
        copy.wait_recv()
    forward(heads_y)
    loads[2].wait()
    loads[3].wait()
    receive(start_y)

    first = gy * lines
    left_at = [jnp.clip(first + i + left_pick[i], 0, ny * lines - 1) - first for i in group]
    right_at = [jnp.clip(first + i + right_pick[i], 0, ny * lines - 1) - first for i in group]

    def keep(k, p):
        for i in group:
            piv[i, k] = p[i].astype(BF16)
            carry[i] = stack_split(p[i])

    def correction(i):
        off = pick(left_at[i], i, half, c_own, c_prev, c_next).astype(F32)
        main = pick(left_at[i], i, half, cd_own, cd_prev, cd_next)
        return jnp.where(on, main[0:1], off)

    keep(2, newton_all([dv[i, 0].astype(F32) - correction(i) for i in group]))

    def step(k, _):
        m, p = advance(
            [dv[i, k] for i in group],
            [ev[i, k - 1, 0] for i in group],
            [ev[i, k - 1, 1] for i in group],
            [carry[i] for i in group],
        )
        for i in group:
            mul[i, k + 1] = m[i].astype(BF16)
        keep(k + 2, p)
        return 0

    middle = tiles // 2
    lax.fori_loop(1, middle, step, 0)
    for copy in rims_x:
        copy.wait_recv()
    forward(rims_y)
    lax.fori_loop(middle, tiles, step, 0)

    receive(heads_y)

    def rim(i, slot):
        refs = (hd_own, hd_prev, hd_next) if slot < 2 else (he_own, he_prev, he_next)
        return pick(right_at[i], i, half, *(ref.at[:, slot % 2] for ref in refs))

    for k in range(2):
        m, p = advance(
            [rim(i, k) for i in group],
            [ev[i, tiles - 1, 0] if k == 0 else rim(i, 2) for i in group],
            [ev[i, tiles - 1, 1] if k == 0 else rim(i, 3) for i in group],
            [carry[i] for i in group],
        )
        for i in group:
            mul[i, tiles + 1 + k] = m[i].astype(BF16)
        keep(tiles + 2 + k, p)

    receive(rims_y)
    for i in group:
        for slot in range(4):
            value = pick(left_at[i], i, half, *(r.at[:, slot] for r in (r_own, r_prev, r_next)))
            if slot < 2:
                piv[i, slot] = value
            else:
                mul[i, slot - 2] = value

    for copy in heads_x + start_x + rims_x:
        copy.wait_send()
    for copies in (start_y, heads_y, rims_y):
        drain(copies)


def on_device(diag_blocks, edge_blocks, left_pick, right_pick):
    lines, tiles, size, _ = diag_blocks.shape
    half = lines // 2
    tile = (size, size)

    def buffers(count):
        return [
            pltpu.VMEM((count,) + tile, BF16),
            pltpu.VMEM((count, 8, size), F32),
            pltpu.VMEM((count, 4) + tile, BF16),
            pltpu.VMEM((count, 2) + tile, BF16),
            pltpu.VMEM((count, 2) + tile, BF16),
        ]

    own, out, prev, nxt = buffers(lines), buffers(lines)[:3], buffers(half), buffers(half)
    vmem = pl.BlockSpec(memory_space=pltpu.VMEM)
    smem = pl.BlockSpec(memory_space=pltpu.SMEM)
    hbm = pl.BlockSpec(memory_space=pl.ANY)
    return pl.pallas_call(
        kernel,
        in_specs=[smem, smem, hbm, hbm],
        out_specs=[vmem, vmem],
        out_shape=[
            jax.ShapeDtypeStruct((lines, tiles + 4) + tile, BF16),
            jax.ShapeDtypeStruct((lines, tiles + 3) + tile, BF16),
        ],
        scratch_shapes=[
            pltpu.VMEM((lines, tiles) + tile, BF16),
            pltpu.VMEM((lines, tiles, 2) + tile, BF16),
            pltpu.VMEM((lines, 2 * size, size), BF16),
        ]
        + out + own + prev + nxt
        + [pltpu.SemaphoreType.DMA((n,)) for n in (4, 9, 9, 10, 10)],
        compiler_params=pltpu.CompilerParams(
            collective_id=0, has_side_effects=True, vmem_limit_bytes=56 * 2**20
        ),
        name="subdomains",
    )(left_pick[:, 0], right_pick[:, 0], diag_blocks, edge_blocks)


def solution(mesh):
    return jax.shard_map(
        on_device,
        mesh=mesh,
        in_specs=(
            P("gy", "gx", None, None),
            P("gy", "gx", None, None, None),
            P("gy", "gx"),
            P("gy", "gx"),
        ),
        out_specs=(P("gy", "gx", None, None), P("gy", "gx", None, None)),
        check_vma=False,
    )
```

time: 288 us -> 75.3 us (0.26)
  the two profiles are of different devices: /device:TPU:19 before, /device:TPU:5 now
where the time goes in v1:
time: 75.3 us; the launch traced here: 75.2 us
  Pallas kernels  68.8 us (91%)
  local copies, waits for them, and re-layouts  5.7 us (8%)
    pallas_call x1, Pallas kernels, on_device(): pl.pallas_call(kernel, in_specs=[smem, smem, hbm, hbm], out_specs=[vmem,...  68.8 us
    unnamed x4, local copies, waits for them, and re-layouts  5.7 us

profile of v1, /device:TPU:5, one launch (start us, length us, event | category | flops | bytes accessed | tf_op | source)
XLA Modules:
  0.0 75.2 jit_solution(12034708624925107362)
XLA Ops:
  0.6 68.8 %subdomains.1 = (bf16[8,12,128,128]{3,2,1,0:T(8,128)(2,1)}, bf16[8,11,128,128]{3,2,1,0:T(8,128)(2,1)}) custom-call(s32[8]{0:T(128)} %bitcast.2, s32[8]{0:T(128)} %bitcast.3, bf16[8,8,128,128]{3,2,1,0:T(8,128)(2,1)} %diag.1, bf16[8,8,2,128,128]{4,3,2,1,0:T(8,128)(2,1)} %edge.1), custom_call_target="tpu_custom_call" | custom-call | tf_op jit(solution)/shard_map/subdomains/pallas_call | solution.py:318
  69.5 0.0 copy-start
  69.5 4.1 %copy.8 = bf16[8,12,128,128]{3,2,1,0:T(8,128)(2,1)} copy(bf16[8,12,128,128]{3,2,1,0:T(8,128)(2,1)} %get-tuple-element.4) | data formatting | bytes 6291456
  73.6 0.0 copy-done
  73.6 1.6 %copy.9 = bf16[8,11,128,128]{3,2,1,0:T(8,128)(2,1)} copy(bf16[8,11,128,128]{3,2,1,0:T(8,128)(2,1)S(1)} %copy-done) | data formatting | bytes 5767168
Async XLA Ops:
  69.5 4.1 %copy-start = (bf16[8,11,128,128]{3,2,1,0:T(8,128)(2,1)S(1)}, bf16[8,11,128,128]{3,2,1,0:T(8,128)(2,1)}, u32[]{:S(2)}) copy-start(bf16[8,11,128,128]{3,2,1,0:T(8,128)(2,1)} %get-tuple-element.5) | copy-start | bytes 8650756

commit v2 on v1

--- a/solution.py
+++ b/solution.py
@@ -85,7 +85,8 @@
     c_own, cd_own, r_own, hd_own, he_own,
     c_prev, cd_prev, r_prev, hd_prev, he_prev,
     c_next, cd_next, r_next, hd_next, he_next,
-    local_sem, send_x, recv_x, send_y, recv_y,
+    relay_a, relay_b,
+    local_sem, send_x, recv_x, send_y, recv_y, send_r, recv_r,
 ):
     lines, tiles, size, _ = dv.shape
     half = lines // 2
@@ -145,13 +146,76 @@
     )
     rims_y = ([to_y(8, r_own.at[low], r_next, up)], [to_y(9, r_own.at[high], r_prev, down)])
 
-    def forward(copies):
-        @pl.when(has_prev)
+    odd = lax.rem(gy, 2) == 1
+    paired = ny % 2 == 0 and ny > 2
+    cross_up = jnp.logical_and(has_prev, jnp.logical_not(odd))
+    cross_down = jnp.logical_and(has_next, odd)
+    two_up, two_down = jnp.maximum(gy - 2, 0), jnp.minimum(gy + 2, ny - 1)
+    front, back = pl.ds(0, 2), pl.ds(2, 2)
+
+    def to_r(a, b, send, recv, y):
+        return pltpu.make_async_remote_copy(
+            src_ref=a, dst_ref=b, send_sem=send, recv_sem=recv,
+            device_id=(gx, y), device_id_type=MESH,
+        )
+
+    heads_r = (
+        [
+            to_r(hd_own.at[low], relay_b.at[:, front], send_y.at[4], recv_r.at[2], down),
+            to_r(he_own.at[low], relay_b.at[:, back], send_y.at[5], recv_r.at[3], down),
+        ],
+        [
+            to_r(hd_own.at[high], relay_a.at[:, front], send_y.at[6], recv_r.at[0], two_down),
+            to_r(he_own.at[high], relay_a.at[:, back], send_y.at[7], recv_r.at[1], two_down),
+        ],
+    )
+    rims_r = (
+        [to_r(r_own.at[low], relay_b, send_y.at[8], recv_r.at[2], two_up)],
+        [to_r(r_own.at[high], relay_a, send_y.at[9], recv_r.at[0], up)],
+    )
+    heads_pass = [
+        to_r(relay_a.at[:, front], hd_prev, send_r.at[0], recv_y.at[6], up),
+        to_r(relay_a.at[:, back], he_prev, send_r.at[1], recv_y.at[7], up),
+        to_r(relay_b.at[:, front], hd_next, send_r.at[2], recv_y.at[4], two_up),
+        to_r(relay_b.at[:, back], he_next, send_r.at[3], recv_y.at[5], two_up),
+    ]
+    rims_pass = [
+        to_r(relay_a, r_prev, send_r.at[0], recv_y.at[9], two_down),
+        to_r(relay_b, r_next, send_r.at[2], recv_y.at[8], down),
+    ]
+    passes_heads = jnp.logical_and(odd, gy > 2)
+    passes_rims = jnp.logical_and(jnp.logical_not(odd), gy + 2 < ny)
+
+    def pass_on(incoming, outgoing, cond):
+        if paired:
+            @pl.when(cond)
+            def _():
+                for copy, onward in zip(incoming[1] + incoming[0], outgoing):
+                    copy.wait_recv()
+                    onward.start()
+
+    def forward(copies, relayed=None):
+        direct_up, direct_down = has_prev, has_next
+        if relayed is not None and paired:
+            direct_up = jnp.logical_and(has_prev, odd)
+            direct_down = jnp.logical_and(has_next, jnp.logical_not(odd))
+
+            @pl.when(cross_down)
+            def _():
+                for copy in relayed[1]:
+                    copy.start()
+
+            @pl.when(cross_up)
+            def _():
+                for copy in relayed[0]:
+                    copy.start()
+
+        @pl.when(direct_up)
         def _():
             for copy in copies[0]:
                 copy.start()
 
-        @pl.when(has_next)
+        @pl.when(direct_down)
         def _():
             for copy in copies[1]:
                 copy.start()
@@ -182,15 +246,18 @@
     for x in (ahead, behind):
         pl.semaphore_signal(barrier, inc=1, device_id=(x, gy), device_id_type=MESH)
 
-    @pl.when(has_prev)
-    def _():
-        pl.semaphore_signal(barrier, inc=1, device_id=(gx, up), device_id_type=MESH)
-
-    @pl.when(has_next)
-    def _():
-        pl.semaphore_signal(barrier, inc=1, device_id=(gx, down), device_id_type=MESH)
-
-    pl.semaphore_wait(barrier, 2 + has_prev.astype(jnp.int32) + has_next.astype(jnp.int32))
+    peers = 2
+    for reach in (1, 2):
+        for there, y in ((gy >= reach, gy - reach), (gy + reach < ny, gy + reach)):
+            peers += there.astype(jnp.int32)
+
+            @pl.when(there)
+            def _():
+                pl.semaphore_signal(
+                    barrier, inc=1, device_id=(gx, jnp.clip(y, 0, ny - 1)), device_id_type=MESH
+                )
+
+    pl.semaphore_wait(barrier, peers)
 
     for copy in heads_x:
         copy.start()
@@ -225,7 +292,7 @@
     forward(start_y)
     for copy in heads_x:
         copy.wait_recv()
-    forward(heads_y)
+    forward(heads_y, heads_r)
     loads[2].wait()
     loads[3].wait()
     receive(start_y)
@@ -260,9 +327,10 @@
 
     middle = tiles // 2
     lax.fori_loop(1, middle, step, 0)
+    pass_on(heads_r, heads_pass, passes_heads)
     for copy in rims_x:
         copy.wait_recv()
-    forward(rims_y)
+    forward(rims_y, rims_r)
     lax.fori_loop(middle, tiles, step, 0)
 
     receive(heads_y)
@@ -282,6 +350,7 @@
             mul[i, tiles + 1 + k] = m[i].astype(BF16)
         keep(tiles + 2 + k, p)
 
+    pass_on(rims_r, rims_pass, passes_rims)
     receive(rims_y)
     for i in group:
         for slot in range(4):
@@ -295,6 +364,13 @@
         copy.wait_send()
     for copies in (start_y, heads_y, rims_y):
         drain(copies)
+    if paired:
+        for cond, copies in ((passes_heads, heads_pass), (passes_rims, rims_pass)):
+
+            @pl.when(cond)
+            def _():
+                for copy in copies:
+                    copy.wait_send()
 
 
 def on_device(diag_blocks, edge_blocks, left_pick, right_pick):
@@ -329,9 +405,10 @@
             pltpu.VMEM((lines, 2 * size, size), BF16),
         ]
         + out + own + prev + nxt
-        + [pltpu.SemaphoreType.DMA((n,)) for n in (4, 9, 9, 10, 10)],
+        + [pltpu.VMEM((half, 4) + tile, BF16)] * 2
+        + [pltpu.SemaphoreType.DMA((n,)) for n in (4, 9, 9, 10, 10, 4, 4)],
         compiler_params=pltpu.CompilerParams(
-            collective_id=0, has_side_effects=True, vmem_limit_bytes=56 * 2**20
+            collective_id=0, has_side_effects=True, vmem_limit_bytes=30 * 2**20
         ),
         name="subdomains",
     )(left_pick[:, 0], right_pick[:, 0], diag_blocks, edge_blocks)

time: 75.3 us -> 68.9 us (0.915)
  the two profiles are of different devices: /device:TPU:5 before, /device:TPU:19 now
where the time goes in v2:
time: 68.9 us; the launch traced here: 68.7 us
  Pallas kernels  59.7 us (87%)
  local copies, waits for them, and re-layouts  8.33 us (12%)
    pallas_call x1, Pallas kernels, on_device(): pl.pallas_call(kernel, in_specs=[smem, smem, hbm, hbm], out_specs=[vmem,...  59.7 us
    unnamed x10, local copies, waits for them, and re-layouts  8.33 us

profile of v2, /device:TPU:19, one launch (start us, length us, event | category | flops | bytes accessed | tf_op | source)
XLA Modules:
  0.0 68.7 jit_solution(7625282749898867554)
XLA Ops:
  0.6 0.0 copy-start
  0.6 2.2 %copy-done = bf16[8,8,2,128,128]{4,3,2,1,0:T(8,128)(2,1)S(1)} copy-done((bf16[8,8,2,128,128]{4,3,2,1,0:T(8,128)(2,1)S(1)}, bf16[8,8,2,128,128]{4,3,2,1,0:T(8,128)(2,1)}, u32[]{:S(2)}) %copy-start) | copy-done | bytes 4194328
  2.8 0.0 copy-start.1
  2.8 1.6 %copy-done.1 = bf16[8,8,128,128]{3,2,1,0:T(8,128)(2,1)S(1)} copy-done((bf16[8,8,128,128]{3,2,1,0:T(8,128)(2,1)S(1)}, bf16[8,8,128,128]{3,2,1,0:T(8,128)(2,1)}, u32[]{:S(2)}) %copy-start.1) | copy-done | bytes 2097176
  4.4 0.0 copy-start.2
  4.4 0.7 copy-done.2
  5.1 0.0 copy-start.3
  5.1 0.7 copy-done.3
  5.7 59.7 %subdomains.1 = (bf16[8,12,128,128]{3,2,1,0:T(8,128)(2,1)S(1)}, bf16[8,11,128,128]{3,2,1,0:T(8,128)(2,1)S(1)}) custom-call(s32[8]{0:T(128)S(1)} %bitcast.2, s32[8]{0:T(128)S(1)} %bitcast.3, bf16[8,8,128,128]{3,2,1,0:T(8,128)(2,1)S(1)} %copy-done.1, bf16[8,8,2,128,128]{4,3,2,1,0:T(8,128)(2,1)S(1)} %copy-done), custom_call_target="tpu_custom_call" | custom-call | tf_op jit(solution)/shard_map/subdomains/pallas_call | solution.py:394
  65.5 1.7 %copy.8 = bf16[8,12,128,128]{3,2,1,0:T(8,128)(2,1)} copy(bf16[8,12,128,128]{3,2,1,0:T(8,128)(2,1)S(1)} %get-tuple-element.4) | data formatting | bytes 6291456
  67.1 1.6 %copy.9 = bf16[8,11,128,128]{3,2,1,0:T(8,128)(2,1)} copy(bf16[8,11,128,128]{3,2,1,0:T(8,128)(2,1)S(1)} %get-tuple-element.5) | data formatting | bytes 5767168
Async XLA Ops:
  0.6 2.2 %copy-start = (bf16[8,8,2,128,128]{4,3,2,1,0:T(8,128)(2,1)S(1)}, bf16[8,8,2,128,128]{4,3,2,1,0:T(8,128)(2,1)}, u32[]{:S(2)}) copy-start(bf16[8,8,2,128,128]{4,3,2,1,0:T(8,128)(2,1)} %edge.1) | copy-start | bytes 12582916
  2.8 1.6 %copy-start.1 = (bf16[8,8,128,128]{3,2,1,0:T(8,128)(2,1)S(1)}, bf16[8,8,128,128]{3,2,1,0:T(8,128)(2,1)}, u32[]{:S(2)}) copy-start(bf16[8,8,128,128]{3,2,1,0:T(8,128)(2,1)} %diag.1) | copy-start | bytes 6291460
  4.4 0.7 copy-start.2
  5.1 0.7 copy-start.3

commit v3 on v2

--- a/solution.py
+++ b/solution.py
@@ -390,7 +390,7 @@
     own, out, prev, nxt = buffers(lines), buffers(lines)[:3], buffers(half), buffers(half)
     vmem = pl.BlockSpec(memory_space=pltpu.VMEM)
     smem = pl.BlockSpec(memory_space=pltpu.SMEM)
-    hbm = pl.BlockSpec(memory_space=pl.ANY)
+    hbm = pl.BlockSpec(memory_space=pltpu.HBM)
     return pl.pallas_call(
         kernel,
         in_specs=[smem, smem, hbm, hbm],
@@ -408,7 +408,7 @@
         + [pltpu.VMEM((half, 4) + tile, BF16)] * 2
         + [pltpu.SemaphoreType.DMA((n,)) for n in (4, 9, 9, 10, 10, 4, 4)],
         compiler_params=pltpu.CompilerParams(
-            collective_id=0, has_side_effects=True, vmem_limit_bytes=30 * 2**20
+            collective_id=0, has_side_effects=True, vmem_limit_bytes=46 * 2**20
         ),
         name="subdomains",
     )(left_pick[:, 0], right_pick[:, 0], diag_blocks, edge_blocks)

time: 68.9 us -> 66.4 us (0.964)
  local copies, waits for them, and re-layouts: 8.33 us -> 6.14 us
    unnamed x10 -> x8, local copies, waits for them, and re-layouts: 8.33 us -> 6.14 us
where the time goes in v3:
time: 66.4 us; the launch traced here: 66.3 us
  Pallas kernels  59.5 us (90%)
  local copies, waits for them, and re-layouts  6.14 us (9%)
    pallas_call x1, Pallas kernels, on_device(): pl.pallas_call(kernel, in_specs=[smem, smem, hbm, hbm], out_specs=[vmem,...  59.5 us
    unnamed x8, local copies, waits for them, and re-layouts  6.14 us

profile of v3, /device:TPU:19, one launch (start us, length us, event | category | flops | bytes accessed | tf_op | source)
XLA Modules:
  0.0 66.3 jit_solution(6870608708348794663)
XLA Ops:
  0.6 0.0 copy-start
  0.6 1.6 %copy-done = bf16[8,8,128,128]{3,2,1,0:T(8,128)(2,1)S(1)} copy-done((bf16[8,8,128,128]{3,2,1,0:T(8,128)(2,1)S(1)}, bf16[8,8,128,128]{3,2,1,0:T(8,128)(2,1)}, u32[]{:S(2)}) %copy-start) | copy-done | bytes 2097176
  2.2 0.0 copy-start.1
  2.2 0.7 copy-done.1
  2.9 0.0 copy-start.2
  2.9 0.7 copy-done.2
  3.5 59.5 %subdomains.1 = (bf16[8,12,128,128]{3,2,1,0:T(8,128)(2,1)S(1)}, bf16[8,11,128,128]{3,2,1,0:T(8,128)(2,1)S(1)}) custom-call(s32[8]{0:T(128)S(1)} %bitcast.2, s32[8]{0:T(128)S(1)} %bitcast.3, bf16[8,8,128,128]{3,2,1,0:T(8,128)(2,1)S(1)} %copy-done, bf16[8,8,2,128,128]{4,3,2,1,0:T(8,128)(2,1)} %edge.1), custom_call_target="tpu_custom_call" | custom-call | tf_op jit(solution)/shard_map/subdomains/pallas_call | solution.py:394
  63.0 1.7 %copy.8 = bf16[8,12,128,128]{3,2,1,0:T(8,128)(2,1)} copy(bf16[8,12,128,128]{3,2,1,0:T(8,128)(2,1)S(1)} %get-tuple-element.4) | data formatting | bytes 6291456
  64.7 1.6 %copy.9 = bf16[8,11,128,128]{3,2,1,0:T(8,128)(2,1)} copy(bf16[8,11,128,128]{3,2,1,0:T(8,128)(2,1)S(1)} %get-tuple-element.5) | data formatting | bytes 5767168
Async XLA Ops:
  0.6 1.6 %copy-start = (bf16[8,8,128,128]{3,2,1,0:T(8,128)(2,1)S(1)}, bf16[8,8,128,128]{3,2,1,0:T(8,128)(2,1)}, u32[]{:S(2)}) copy-start(bf16[8,8,128,128]{3,2,1,0:T(8,128)(2,1)} %diag.1) | copy-start | bytes 6291460
  2.2 0.7 copy-start.1
  2.9 0.7 copy-start.2
